TPU v7x, 128 devices: a whole 4x4x4 slice. The times are simulated.
128 devices in a mesh: prow: 16 (over z, x), pcol: 8 (over y, core).
Axes of the slice: x: 4, y: 4, z: 4, core: 2. Of those that a mesh axis runs over, the one named last changes fastest.
Arguments:
- kernel_tiles: float32 [4, 16, 256, 8, 8, 256], P(None, 'prow', None, None, 'pcol'), may hold values from 0 to 11, as said below
Outputs:
- factored: float32 [4, 16, 256, 8, 8, 256], P(None, 'prow', None, None, 'pcol')
Inputs may be any that keep to these rules, and one draw needn't show every extreme that they name: kernel_tiles is a symmetric positive definite matrix in the stated layout: a product of two exponential covariances of locations and times, scaled per point, plus a diagonal term of at least 0.5.
All inputs are finite; a program needn't handle non-finite values.
Results may differ from a plain program's by a relative error of at most 0.000061.
Values sent between devices are 32-bit elements; how exact they have to be, the bound alone decides.
A program may use at most 128 MiB of HBM per device.

v0:
```python
import jax
import jax.numpy as jnp
from jax import lax
from jax.sharding import PartitionSpec as P

highest = lax.Precision.HIGHEST


def picked(shard, axis, root):
    return lax.dynamic_index_in_dim(lax.all_gather(shard, axis), root, 0, keepdims=False)


def from_root(shard, axis, root):
    mine = lax.axis_index(axis) == root
    return lax.psum(jnp.where(mine, shard, jnp.zeros_like(shard)), axis)


def tile_solve(factor, tile_rows):
    tile_count, tile_width, _ = tile_rows.shape
    flat_rows = tile_rows.reshape(tile_count * tile_width, tile_width)
    solved = jax.scipy.linalg.solve_triangular(factor, flat_rows.T, lower=True)
    return solved.T.reshape(tile_count, tile_width, tile_width)


def factor_panel(local_block, panel_index, global_rows):
    procs_row = lax.axis_size("prow")
    procs_col = lax.axis_size("pcol")
    tile_row = panel_index // procs_row
    tile_col = panel_index // procs_col
    factor = jnp.linalg.cholesky(local_block[tile_row, :, tile_col, :])
    factor = picked(factor, "prow", panel_index % procs_row)
    solved = tile_solve(factor, local_block[:, :, tile_col, :])
    lower_rows = (global_rows > panel_index)[:, None, None]
    diag_rows = (global_rows == panel_index)[:, None, None]
    panel = jnp.where(lower_rows, solved, jnp.where(diag_rows, factor[None], jnp.float32(0.0)))
    row_panel = picked(panel, "pcol", panel_index % procs_col)
    return (panel, row_panel)


def column_tiles(row_panel):
    procs_row = lax.axis_size("prow")
    tile_width = row_panel.shape[1]
    procs_col = lax.axis_size("pcol")
    multiple = procs_row // procs_col
    col_index = lax.axis_index("pcol")
    received = []
    for owner_step in range(multiple):
        received.append(from_root(row_panel, "prow", col_index + owner_step * procs_col))
    stacked = jnp.stack(received, axis=1)
    return stacked.reshape(-1, tile_width, tile_width)


def trailing(local_block, lead, global_rows, global_cols, row_panel, col_panel):
    update = jnp.einsum("arn,csn->arcs", row_panel, col_panel, precision=highest)
    active = (global_rows > lead)[:, None, None, None] & (global_cols > lead)[None, None, :, None]
    return jnp.where(active, local_block - update, local_block)


def write_panel(local_block, panel_index, panel, global_rows, global_cols):
    in_column = (global_cols == panel_index)[None, None, :, None]
    result = jnp.where(in_column, panel[:, :, None, :], local_block)
    upper = (global_rows == panel_index)[:, None, None, None] & (global_cols > panel_index)[
        None, None, :, None
    ]
    return jnp.where(upper, jnp.float32(0.0), result)


def shards(kernel_tiles):
    row_count, _, tile_width, col_count, _, _ = kernel_tiles.shape
    local_block = kernel_tiles.reshape(row_count, tile_width, col_count, tile_width)
    global_rows = jnp.arange(row_count, dtype=jnp.int32) * lax.axis_size("prow") + lax.axis_index(
        "prow"
    )
    global_cols = jnp.arange(col_count, dtype=jnp.int32) * lax.axis_size("pcol") + lax.axis_index(
        "pcol"
    )
    panel_zero, rows_zero = factor_panel(local_block, 0, global_rows)
    cols_zero = column_tiles(rows_zero)
    result = trailing(local_block, 0, global_rows, global_cols, rows_zero, cols_zero)
    result = write_panel(result, 0, panel_zero, global_rows, global_cols)
    panel_one, rows_one = factor_panel(result, 1, global_rows)
    cols_one = column_tiles(rows_one)
    result = trailing(result, 1, global_rows, global_cols, rows_one, cols_one)
    result = write_panel(result, 1, panel_one, global_rows, global_cols)
    return result.reshape(kernel_tiles.shape)


def solution(mesh):
    in_specs = (P(None, "prow", None, None, "pcol", None),)
    out_specs = P(None, "prow", None, None, "pcol", None)
    return jax.shard_map(shards, mesh=mesh, in_specs=in_specs, out_specs=out_specs, check_vma=False)
```

profile of v0, /device:TPU:0, one launch (start us, length us, event | category | flops | bytes accessed | tf_op | source)
XLA Modules:
  0.0 611.4 jit_solution(7833220030949401913)
XLA Ops:
  6.5 20.5 %copy.31 = f32[4,1,256,8,1,256]{2,5,3,0,4,1:T(8,128)} copy(f32[4,1,256,8,1,256]{5,4,3,2,1,0:T(1,128)} %param.4) | data formatting | bytes 16777216 | tf_op args[0]
  27.1 1.0 slice_bitcast_fusion.1
  28.2 1.0 fusion.18
  29.2 11.7 %cholesky.130 = f32[128,128]{1,0:T(8,128)S(1)} custom-call(f32[128,128]{1,0:T(8,128)S(1)} %cholesky.194), custom_call_target="Cholesky" | custom-call | tf_op jit(solution)/shard_map/jit(cholesky)/cholesky | solution.py:30
  41.0 9.8 %custom-call.13 = f32[1,128,128]{1,2,0:T(8,128)S(1)} custom-call(f32[1,128,128]{2,1,0:T(8,128)S(1)} %get-tuple-element.62), custom_call_target="InvertDiagBlocksLowerTriangular" | custom-call | tf_op jit(solution)/shard_map/jit(cholesky)/cholesky | solution.py:30
  51.0 0.3 convolution_subtract_fusion.3
  51.3 11.7 %cholesky.147 = f32[128,128]{1,0:T(8,128)S(1)} custom-call(f32[128,128]{1,0:T(8,128)S(1)} %convolution_subtract_fusion.3), custom_call_target="Cholesky" | custom-call | tf_op jit(solution)/shard_map/jit(cholesky)/cholesky | solution.py:30
  63.0 0.7 compare_reduce_fusion.2
  64.9 0.7 fusion.19
  65.6 0.5 all-gather.7.cloned.1.call-start
  66.1 1.3 slice.70
  67.5 0.3 copy.33
  67.8 0.3 copy.34
  68.2 51.7 %all-gather.11.cloned.1.call-done = f32[4096,256]{1,0:T(8,128)} async-done(((f32[256,256]{1,0:T(8,128)}), f32[4096,256]{1,0:T(8,128)}) %all-gather.11.cloned.1.call-update) | async-done | bytes 4194320 | tf_op jit(solution)/shard_map/all_gather | solution.py:10
  119.9 1.0 fusion.40
  121.0 3.8 while.4
  121.0 0.6 fusion.53
  121.6 1.3 bitcast_dynamic-update-slice_fusion.4
  122.9 0.6 fusion.53
  123.5 1.3 bitcast_dynamic-update-slice_fusion.4
  124.8 19.7 %custom-call.14 = f32[2,128,128]{1,2,0:T(8,128)S(1)} custom-call(f32[2,128,128]{2,1,0:T(8,128)S(1)} %get-tuple-element.21), custom_call_target="InvertDiagBlocksLowerTriangular" | custom-call | tf_op jit(solution)/shard_map/jit(_solve_triangular)/triangular_solve | solution.py:21
  144.5 0.6 fusion.15
  145.1 0.6 convolution_subtract_fusion.1
  145.7 0.6 fusion.28
  146.5 0.3 copy.53
  146.8 1.3 select_select_fusion.2
  148.1 49.4 %all-gather.7.cloned.1.call-done = f32[8,4,256,256]{3,2,1,0:T(8,128)} async-done(((f32[1,4,256,256]{3,2,1,0:T(8,128)}), f32[8,4,256,256]{3,2,1,0:T(8,128)}) %all-gather.7.cloned.1.call-update) | async-done | bytes 8388624 | tf_op jit(solution)/shard_map/all_gather | solution.py:10
  197.5 2.8 fusion.9
  200.7 0.3 copy.36
  201.0 90.6 %all-reduce.8.cloned.1.call-done = (f32[4,1,256,256]{3,2,0,1:T(8,128)}, f32[4,1,256,256]{3,2,0,1:T(8,128)}) async-done(((f32[4,1,256,256]{3,2,0,1:T(8,128)}, f32[4,1,256,256]{3,2,0,1:T(8,128)}), (f32[4,1,256,256]{3,2,0,1:T(8,128)}, f32[4,1,256,256]{3,2,0,1:T(8,128)})) %all-reduce.8.cloned.1.call-update) | async-done | bytes 2097168 | tf_op jit(solution)/shard_map/psum | solution.py:15
  291.6 1.7 pad_maximum_fusion
  293.4 11.1 %fusion.1 = f32[4,256,8,256]{1,3,2,0:T(8,128)S(1)} fusion(f32[4,256,256]{1,2,0:T(8,128)S(1)} %copy.36, pred[8]{0:T(512)(128)(4,1)S(1)} %broadcast_compare_fusion, pred[4,8]{1,0:T(4,128)(4,1)S(1)} %get-tuple-element.66, pred[4,8]{1,0:T(4,128)(4,1)S(1)} %get-tuple-element.65, f32[8,256,256,1]{2,1,0,3:T(8,128)S(1)} %bitcast.131, ...), kind=kOutput, calls=%fused_computation.7 | convolution fusion | flops 6450839552 | bytes 20971592 | tf_op jit(solution)/shard_map/arn,csn->arcs/dot_general | solution.py:54
  304.5 3.4 copy-done
  308.1 1.0 fusion.17
  309.1 11.7 %cholesky.164 = f32[128,128]{1,0:T(8,128)S(1)} custom-call(f32[128,128]{1,0:T(8,128)S(1)} %cholesky.197), custom_call_target="Cholesky" | custom-call | tf_op jit(solution)/shard_map/jit(cholesky)/cholesky | solution.py:30
  320.8 9.8 %custom-call.15 = f32[1,128,128]{1,2,0:T(8,128)S(1)} custom-call(f32[1,128,128]{2,1,0:T(8,128)S(1)} %get-tuple-element.58), custom_call_target="InvertDiagBlocksLowerTriangular" | custom-call | tf_op jit(solution)/shard_map/jit(cholesky)/cholesky | solution.py:30
  330.9 0.3 convolution_subtract_fusion.2
  331.1 11.7 %cholesky.181 = f32[128,128]{1,0:T(8,128)S(1)} custom-call(f32[128,128]{1,0:T(8,128)S(1)} %convolution_subtract_fusion.2), custom_call_target="Cholesky" | custom-call | tf_op jit(solution)/shard_map/jit(cholesky)/cholesky | solution.py:30
  342.9 0.6 compare_reduce_fusion.1
  343.5 0.7 compare_reduce_fusion
  345.4 0.7 fusion.21
  346.2 1.3 slice.73
  347.5 0.3 copy.41
  347.9 0.3 copy.42
  348.2 49.3 %all-gather.13.cloned.1.call-done = f32[4096,256]{1,0:T(8,128)} async-done(((f32[256,256]{1,0:T(8,128)}), f32[4096,256]{1,0:T(8,128)}) %all-gather.13.cloned.1.call-update) | async-done | bytes 4194320 | tf_op jit(solution)/shard_map/all_gather | solution.py:10
  397.5 1.0 fusion.39
  398.5 4.0 while.5
  398.7 0.6 fusion.54
  399.3 1.3 bitcast_dynamic-update-slice_fusion.5
  400.6 0.6 fusion.54
  401.2 1.3 bitcast_dynamic-update-slice_fusion.5
  402.5 19.7 %custom-call.16 = f32[2,128,128]{1,2,0:T(8,128)S(1)} custom-call(f32[2,128,128]{2,1,0:T(8,128)S(1)} %get-tuple-element.22), custom_call_target="InvertDiagBlocksLowerTriangular" | custom-call | tf_op jit(solution)/shard_map/jit(_solve_triangular)/triangular_solve | solution.py:21
  422.2 0.6 fusion.13
  422.8 0.6 convolution_subtract_fusion
  423.4 0.6 fusion.24
  424.2 0.3 copy.43
  424.5 1.3 select_select_fusion
  425.8 49.4 %all-gather.9.cloned.1.call-done = f32[8,4,256,256]{3,2,1,0:T(8,128)} async-done(((f32[1,4,256,256]{3,2,1,0:T(8,128)}), f32[8,4,256,256]{3,2,1,0:T(8,128)}) %all-gather.9.cloned.1.call-update) | async-done | bytes 8388624 | tf_op jit(solution)/shard_map/all_gather | solution.py:10
  475.2 2.8 fusion.7
  478.3 0.3 copy.44
  478.6 90.9 %all-reduce.6.cloned.1.call-done = (f32[4,1,256,256]{3,2,0,1:T(8,128)}, f32[4,1,256,256]{3,2,0,1:T(8,128)}) async-done(((f32[4,1,256,256]{3,2,0,1:T(8,128)}, f32[4,1,256,256]{3,2,0,1:T(8,128)}), (f32[4,1,256,256]{3,2,0,1:T(8,128)}, f32[4,1,256,256]{3,2,0,1:T(8,128)})) %all-reduce.6.cloned.1.call-update) | async-done | bytes 2097168 | tf_op jit(solution)/shard_map/psum | solution.py:15
  569.5 1.7 pad_maximum_fusion.1
  571.4 12.4 %fusion.4 = f32[4,1,256,8,1,256]{2,5,3,0,4,1:T(8,128)} fusion(f32[4,256,8,256]{1,3,2,0:T(8,128)} %copy-done, f32[4,256,256]{1,2,0:T(8,128)S(1)} %copy.44, pred[8]{0:T(512)(128)(4,1)S(1)} %broadcast_compare_fusion.4, pred[4,8]{1,0:T(4,128)(4,1)S(1)} %get-tuple-element.64, pred[4,8]{1,0:T(4,128)(4,1)S(1)} %get-tuple-element.63, ...), kind=kOutput, calls=%fused_computation.10 | convolution fusion | flops 6450839552 | bytes 20971592 | tf_op jit(solution)/shard_map/arn,csn->arcs/dot_general | solution.py:54
  583.8 20.5 %copy.48 = f32[4,1,256,8,1,256]{5,4,3,2,1,0:T(1,128)} copy(f32[4,1,256,8,1,256]{2,5,3,0,4,1:T(8,128)} %fusion.4) | data formatting | bytes 16777216 | tf_op jit(solution)/shard_map/reshape | solution.py:85
  (46 shorter events, 2.3 us)
Async XLA Ops:
  6.5 113.4 %all-gather.11.cloned.1.call-start = ((), (), s32[]{:S(2)}) async-start(), calls=%async_computation.2 | async-start | bytes 4456448 | tf_op jit(solution)/shard_map/all_gather | solution.py:10
  65.6 131.9 %all-gather.7.cloned.1.call-start = ((), (), s32[]{:S(2)}) async-start(), calls=%async_computation | async-start | bytes 9437184 | tf_op jit(solution)/shard_map/all_gather | solution.py:10
  148.1 143.5 %all-reduce.8.cloned.1.call-start = ((), (), s32[]{:S(2)}) async-start(), calls=%async_computation.5 | async-start | bytes 4194304 | tf_op jit(solution)/shard_map/psum | solution.py:15
  200.3 197.1 %all-gather.13.cloned.1.call-start = ((), (), s32[]{:S(2)}) async-start(), calls=%async_computation.3 | async-start | bytes 4456448 | tf_op jit(solution)/shard_map/all_gather | solution.py:10
  304.5 3.4 copy-start
  346.1 129.1 %all-gather.9.cloned.1.call-start = ((), (), s32[]{:S(2)}) async-start(), calls=%async_computation.1 | async-start | bytes 9437184 | tf_op jit(solution)/shard_map/all_gather | solution.py:10
  425.8 143.7 %all-reduce.6.cloned.1.call-start = ((), (), s32[]{:S(2)}) async-start(), calls=%async_computation.4 | async-start | bytes 4194304 | tf_op jit(solution)/shard_map/psum | solution.py:15
Sparse Core Ops, SparseCore 0:
  65.8 54.1 all-gather.10
  148.2 49.2 all-gather.6
  201.0 90.5 all-reduce.7
  346.3 51.1 all-gather.12
  425.9 49.2 all-gather.8
  478.9 90.6 all-reduce.5
where the time goes:
time: 621 us; the launch traced here: 611 us
  waiting for transfers between devices  381 us (61%)
  other arithmetic  125 us (20%)
  local copies, waits for them, and re-layouts  58.9 us (9%)
  matrix products  28.1 us (5%)
  between operations  16.5 us (3%)
    all_gather x4, waiting for transfers between devices, picked(): lax.all_gather(shard, axis)  200 us
    psum x2, waiting for transfers between devices, from_root(): return lax.psum(jnp.where(mine, shard, jnp.zeros_like(shard)), axis)  181 us
    another operation x13, other arithmetic, factor_panel(): factor = jnp.linalg.cholesky(local_block[tile_row, :, tile_col, :])  68.6 us
    another operation x3, other arithmetic, tile_solve(): solved = jax.scipy.linalg.solve_triangular(factor, flat_rows.T, lower=True)  39.4 us
    unnamed x3, local copies, waits for them, and re-layouts  23.9 us
    dot_general x2, matrix products, trailing(): jnp.einsum('arn,csn->arcs', row_panel, col_panel, precision=highest)  23.5 us
    reshape x1, local copies, waits for them, and re-layouts, shards(): return result.reshape(kernel_tiles.shape)  20.5 us
  transfers between devices with their start and end apart: 6, of which 6 were waited for; matrix products, arithmetic and copies ran while one was open for 1% of the time, Pallas kernels for 0%

commit v1 on v0

--- a/solution.py
+++ b/solution.py
@@ -6,13 +6,17 @@
 highest = lax.Precision.HIGHEST
 
 
+def trace_task(load, mesh_name):
+    return lax.all_gather(load, axis_name=mesh_name).sum(axis=0)
+
+
 def picked(shard, axis, root):
     return lax.dynamic_index_in_dim(lax.all_gather(shard, axis), root, 0, keepdims=False)
 
 
 def from_root(shard, axis, root):
     mine = lax.axis_index(axis) == root
-    return lax.psum(jnp.where(mine, shard, jnp.zeros_like(shard)), axis)
+    return trace_task(jnp.where(mine, shard, jnp.zeros_like(shard)), axis)
 
 
 def tile_solve(factor, tile_rows):

time: 621 us -> 900 us (1.45)
  waiting for transfers between devices: 381 us -> 635 us
  other arithmetic: 125 us -> 151 us
    all_gather x0 -> x4, waiting for transfers between devices: none -> 434 us  [trace_task(): return lax.all_gather(load, axis_name=mesh_name).sum(axis=0)]
    psum x2 -> x0, waiting for transfers between devices: 181 us -> none  [from_root(): return lax.psum(jnp.where(mine, shard, jnp.zeros_like(shard)), axis)]
    reduce_sum x0 -> x4, other arithmetic: none -> 28 us  [trace_task(): return lax.all_gather(load, axis_name=mesh_name).sum(axis=0)]
  transfers between devices with their start and end apart: 6 -> 8, of which waited for: 6 -> 8; matrix products, arithmetic and copies ran while one was open for 1% -> 2% of each run, Pallas kernels for 0% -> 0%
where the time goes in v1:
time: 900 us; the launch traced here: 890 us
  waiting for transfers between devices  635 us (71%)
  other arithmetic  151 us (17%)
  local copies, waits for them, and re-layouts  58.7 us (7%)
  matrix products  28.1 us (3%)
  between operations  16.7 us (2%)
    all_gather x4, waiting for transfers between devices, trace_task(): return lax.all_gather(load, axis_name=mesh_name).sum(axis=0)  434 us
    all_gather x4, waiting for transfers between devices, picked(): lax.all_gather(shard, axis)  200 us
    another operation x13, other arithmetic, factor_panel(): factor = jnp.linalg.cholesky(local_block[tile_row, :, tile_col, :])  68.7 us
    another operation x3, other arithmetic, tile_solve(): solved = jax.scipy.linalg.solve_triangular(factor, flat_rows.T, lower=True)  39.4 us
    reduce_sum x4, other arithmetic, trace_task(): return lax.all_gather(load, axis_name=mesh_name).sum(axis=0)  28 us
    unnamed x3, local copies, waits for them, and re-layouts  23.9 us
    dot_general x2, matrix products, trailing(): jnp.einsum('arn,csn->arcs', row_panel, col_panel, precision=highest)  23.5 us
    reshape x1, local copies, waits for them, and re-layouts, shards(): return result.reshape(kernel_tiles.shape)  20.5 us
  transfers between devices with their start and end apart: 8, of which 8 were waited for; matrix products, arithmetic and copies ran while one was open for 2% of the time, Pallas kernels for 0%

profile of v1, /device:TPU:0, one launch (start us, length us, event | category | flops | bytes accessed | tf_op | source)
XLA Modules:
  0.0 890.2 jit_solution(53640242560959556)
XLA Ops:
  6.5 20.5 %copy.28 = f32[4,1,256,8,1,256]{2,5,3,0,4,1:T(8,128)} copy(f32[4,1,256,8,1,256]{5,4,3,2,1,0:T(1,128)} %param.4) | data formatting | bytes 16777216 | tf_op args[0]
  27.1 1.0 slice_bitcast_fusion.1
  28.2 1.0 fusion.14
  29.2 11.7 %cholesky.130 = f32[128,128]{1,0:T(8,128)S(1)} custom-call(f32[128,128]{1,0:T(8,128)S(1)} %cholesky.194), custom_call_target="Cholesky" | custom-call | tf_op jit(solution)/shard_map/jit(cholesky)/cholesky | solution.py:34
  41.0 9.8 %custom-call.13 = f32[1,128,128]{1,2,0:T(8,128)S(1)} custom-call(f32[1,128,128]{2,1,0:T(8,128)S(1)} %get-tuple-element.62), custom_call_target="InvertDiagBlocksLowerTriangular" | custom-call | tf_op jit(solution)/shard_map/jit(cholesky)/cholesky | solution.py:34
  51.3 11.7 %cholesky.147 = f32[128,128]{1,0:T(8,128)S(1)} custom-call(f32[128,128]{1,0:T(8,128)S(1)} %convolution_subtract_fusion.3), custom_call_target="Cholesky" | custom-call | tf_op jit(solution)/shard_map/jit(cholesky)/cholesky | solution.py:34
  63.0 0.7 compare_reduce_fusion.2
  65.0 0.7 fusion.15
  65.7 0.5 all-gather.11.cloned.1.call-start
  66.2 1.3 slice.70
  67.6 0.3 copy.30
  67.9 0.3 copy.31
  68.3 51.7 %all-gather.23.cloned.1.call-done = f32[4096,256]{1,0:T(8,128)} async-done(((f32[256,256]{1,0:T(8,128)}), f32[4096,256]{1,0:T(8,128)}) %all-gather.23.cloned.1.call-update) | async-done | bytes 4194320 | tf_op jit(solution)/shard_map/all_gather | solution.py:14
  120.0 1.0 fusion.38
  121.1 4.1 while.4
  121.1 0.6 fusion.51
  121.8 1.3 bitcast_dynamic-update-slice_fusion.4
  123.1 0.6 fusion.51
  123.8 1.3 bitcast_dynamic-update-slice_fusion.4
  125.2 19.7 %custom-call.14 = f32[2,128,128]{1,2,0:T(8,128)S(1)} custom-call(f32[2,128,128]{2,1,0:T(8,128)S(1)} %get-tuple-element.21), custom_call_target="InvertDiagBlocksLowerTriangular" | custom-call | tf_op jit(solution)/shard_map/jit(_solve_triangular)/triangular_solve | solution.py:25
  144.8 0.6 fusion.11
  145.5 0.6 convolution_subtract_fusion.1
  146.1 0.6 fusion.24
  147.0 0.3 copy.48
  147.3 1.2 select_select_fusion.1
  148.5 49.4 %all-gather.11.cloned.1.call-done = f32[8,4,256,256]{3,2,1,0:T(8,128)} async-done(((f32[1,4,256,256]{3,2,1,0:T(8,128)}), f32[8,4,256,256]{3,2,1,0:T(8,128)}) %all-gather.11.cloned.1.call-update) | async-done | bytes 8388624 | tf_op jit(solution)/shard_map/all_gather | solution.py:14
  197.9 2.8 slice_select_fusion.3
  200.8 0.5 all-gather.13.cloned.1.call-update
  201.8 110.7 %all-gather.15.cloned.1.call-done = f32[16,4,256,256]{3,2,1,0:T(8,128)} async-done(((f32[1,4,256,256]{3,2,1,0:T(8,128)}), f32[16,4,256,256]{3,2,1,0:T(8,128)}) %all-gather.15.cloned.1.call-update) | async-done | bytes 16777232 | tf_op jit(solution)/shard_map/all_gather | solution.py:10
  312.5 7.0 reduce_sum.37
  319.5 106.1 %all-gather.13.cloned.1.call-done = f32[16,4,256,256]{3,2,1,0:T(8,128)} async-done(((f32[1,4,256,256]{3,2,1,0:T(8,128)}), f32[16,4,256,256]{3,2,1,0:T(8,128)}) %all-gather.13.cloned.1.call-update) | async-done | bytes 16777232 | tf_op jit(solution)/shard_map/all_gather | solution.py:10
  425.6 7.0 reduce_sum.36
  432.8 11.1 %fusion.1 = f32[4,256,8,256]{1,3,2,0:T(8,128)S(1)} fusion(f32[4,256,256]{1,2,0:T(8,128)S(1)} %bitcast_select_fusion.1, pred[8]{0:T(512)(128)(4,1)S(1)} %broadcast_compare_fusion, pred[4,8]{1,0:T(4,128)(4,1)S(1)} %get-tuple-element.66, pred[4,8]{1,0:T(4,128)(4,1)S(1)} %get-tuple-element.65, f32[8,256,256,1]{2,1,0,3:T(8,128)S(1)} %bitcast.115, ...), kind=kOutput, calls=%fused_computation.7 | convolution fusion | flops 6450839552 | bytes 20971592 | tf_op jit(solution)/shard_map/arn,csn->arcs/dot_general | solution.py:58
  443.9 3.4 copy-done
  447.5 1.0 fusion.13
  448.5 11.7 %cholesky.164 = f32[128,128]{1,0:T(8,128)S(1)} custom-call(f32[128,128]{1,0:T(8,128)S(1)} %cholesky.197), custom_call_target="Cholesky" | custom-call | tf_op jit(solution)/shard_map/jit(cholesky)/cholesky | solution.py:34
  460.3 9.8 %custom-call.15 = f32[1,128,128]{1,2,0:T(8,128)S(1)} custom-call(f32[1,128,128]{2,1,0:T(8,128)S(1)} %get-tuple-element.58), custom_call_target="InvertDiagBlocksLowerTriangular" | custom-call | tf_op jit(solution)/shard_map/jit(cholesky)/cholesky | solution.py:34
  470.6 11.7 %cholesky.181 = f32[128,128]{1,0:T(8,128)S(1)} custom-call(f32[128,128]{1,0:T(8,128)S(1)} %convolution_subtract_fusion.2), custom_call_target="Cholesky" | custom-call | tf_op jit(solution)/shard_map/jit(cholesky)/cholesky | solution.py:34
  482.3 0.7 compare_reduce_fusion.1
  483.0 0.7 compare_reduce_fusion
  484.9 0.7 fusion.17
  485.8 1.3 slice.73
  487.7 49.3 %all-gather.25.cloned.1.call-done = f32[4096,256]{1,0:T(8,128)} async-done(((f32[256,256]{1,0:T(8,128)}), f32[4096,256]{1,0:T(8,128)}) %all-gather.25.cloned.1.call-update) | async-done | bytes 4194320 | tf_op jit(solution)/shard_map/all_gather | solution.py:14
  537.1 1.0 fusion.37
  538.1 4.3 while.5
  538.3 0.6 fusion.52
  539.0 1.3 bitcast_dynamic-update-slice_fusion.5
  540.4 0.6 fusion.52
  541.0 1.3 bitcast_dynamic-update-slice_fusion.5
  542.4 19.7 %custom-call.16 = f32[2,128,128]{1,2,0:T(8,128)S(1)} custom-call(f32[2,128,128]{2,1,0:T(8,128)S(1)} %get-tuple-element.22), custom_call_target="InvertDiagBlocksLowerTriangular" | custom-call | tf_op jit(solution)/shard_map/jit(_solve_triangular)/triangular_solve | solution.py:25
  562.1 0.6 fusion.9
  562.7 0.6 convolution_subtract_fusion
  563.3 0.6 fusion.20
  564.2 0.3 copy.41
  564.5 1.2 select_select_fusion
  565.8 49.4 %all-gather.17.cloned.1.call-done = f32[8,4,256,256]{3,2,1,0:T(8,128)} async-done(((f32[1,4,256,256]{3,2,1,0:T(8,128)}), f32[8,4,256,256]{3,2,1,0:T(8,128)}) %all-gather.17.cloned.1.call-update) | async-done | bytes 8388624 | tf_op jit(solution)/shard_map/all_gather | solution.py:14
  615.2 2.8 slice_select_fusion.1
  618.0 0.7 all-gather.19.cloned.1.call-update
  619.1 110.6 %all-gather.21.cloned.1.call-done = f32[16,4,256,256]{3,2,1,0:T(8,128)} async-done(((f32[1,4,256,256]{3,2,1,0:T(8,128)}), f32[16,4,256,256]{3,2,1,0:T(8,128)}) %all-gather.21.cloned.1.call-update) | async-done | bytes 16777232 | tf_op jit(solution)/shard_map/all_gather | solution.py:10
  729.8 7.0 reduce_sum.39
  736.8 106.2 %all-gather.19.cloned.1.call-done = f32[16,4,256,256]{3,2,1,0:T(8,128)} async-done(((f32[1,4,256,256]{3,2,1,0:T(8,128)}), f32[16,4,256,256]{3,2,1,0:T(8,128)}) %all-gather.19.cloned.1.call-update) | async-done | bytes 16777232 | tf_op jit(solution)/shard_map/all_gather | solution.py:10
  843.0 7.0 reduce_sum.38
  850.2 12.4 %fusion.4 = f32[4,1,256,8,1,256]{2,5,3,0,4,1:T(8,128)} fusion(f32[4,256,8,256]{1,3,2,0:T(8,128)} %copy-done, f32[4,256,256]{1,2,0:T(8,128)S(1)} %bitcast_select_fusion, pred[8]{0:T(512)(128)(4,1)S(1)} %broadcast_compare_fusion.4, pred[4,8]{1,0:T(4,128)(4,1)S(1)} %get-tuple-element.64, pred[4,8]{1,0:T(4,128)(4,1)S(1)} %get-tuple-element.63, ...), kind=kOutput, calls=%fused_computation.10 | convolution fusion | flops 6450839552 | bytes 20971592 | tf_op jit(solution)/shard_map/arn,csn->arcs/dot_general | solution.py:58
  862.6 20.5 %copy.43 = f32[4,1,256,8,1,256]{5,4,3,2,1,0:T(1,128)} copy(f32[4,1,256,8,1,256]{2,5,3,0,4,1:T(8,128)} %fusion.4) | data formatting | bytes 16777216 | tf_op jit(solution)/shard_map/reshape | solution.py:89
  (54 shorter events, 4.3 us)
Async XLA Ops:
  6.5 113.5 %all-gather.23.cloned.1.call-start = ((), (), s32[]{:S(2)}) async-start(), calls=%async_computation.6 | async-start | bytes 4456448 | tf_op jit(solution)/shard_map/all_gather | solution.py:14
  65.7 132.2 %all-gather.11.cloned.1.call-start = ((), (), s32[]{:S(2)}) async-start(), calls=%async_computation | async-start | bytes 9437184 | tf_op jit(solution)/shard_map/all_gather | solution.py:14
  148.5 164.1 %all-gather.15.cloned.1.call-start = ((), (), s32[]{:S(2)}) async-start(), calls=%async_computation.2 | async-start | bytes 17825792 | tf_op jit(solution)/shard_map/all_gather | solution.py:10
  200.8 224.9 %all-gather.13.cloned.1.call-start = ((), (), s32[]{:S(2)}) async-start(), calls=%async_computation.1 | async-start | bytes 17825792 | tf_op jit(solution)/shard_map/all_gather | solution.py:10
  201.3 335.8 %all-gather.25.cloned.1.call-start = ((), (), s32[]{:S(2)}) async-start(), calls=%async_computation.7 | async-start | bytes 4456448 | tf_op jit(solution)/shard_map/all_gather | solution.py:14
  443.9 3.4 copy-start
  485.7 129.5 %all-gather.17.cloned.1.call-start = ((), (), s32[]{:S(2)}) async-start(), calls=%async_computation.3 | async-start | bytes 9437184 | tf_op jit(solution)/shard_map/all_gather | solution.py:14
  565.7 164.1 %all-gather.21.cloned.1.call-start = ((), (), s32[]{:S(2)}) async-start(), calls=%async_computation.5 | async-start | bytes 17825792 | tf_op jit(solution)/shard_map/all_gather | solution.py:10
  618.0 225.0 %all-gather.19.cloned.1.call-start = ((), (), s32[]{:S(2)}) async-start(), calls=%async_computation.4 | async-start | bytes 17825792 | tf_op jit(solution)/shard_map/all_gather | solution.py:10
Sparse Core Ops, SparseCore 0:
  65.9 54.1 all-gather.22
  148.6 49.2 all-gather.10
  200.9 111.6 all-gather.14
  314.5 111.0 all-gather.12
  485.8 51.2 all-gather.24
  565.8 49.2 all-gather.16
  618.1 111.6 all-gather.20
  731.9 111.0 all-gather.18
